TPU v7x, 512 devices: a whole 4x8x8 slice. The times are simulated.
512 devices in a mesh: segment: 4 (over x), chan: 16 (over y, core), dp: 8 (over z).
Axes of the slice: x: 4, y: 8, z: 8, core: 2. Of those that a mesh axis runs over, the one named last changes fastest.
Arguments:
- grad_top: bfloat16 [8, 1536, 256], P('dp', None, 'chan'), may hold values from -6 to 6
- inputs_one: bfloat16 [4, 8, 1536, 256], P('segment', 'dp', 'chan'), may hold values from -6 to 6
- conv_one: bfloat16 [4, 8, 1536, 256], P('segment', 'dp', 'chan'), may hold values from -130 to 130
- inputs_two: bfloat16 [4, 8, 1536, 256], P('segment', 'dp', 'chan'), may hold values from -6 to 6
- conv_two: bfloat16 [4, 8, 1536, 256], P('segment', 'dp', 'chan'), may hold values from -130 to 130
- proj_weight: bfloat16 [4, 2, 1536, 1536], P('segment', None, 'chan'), may hold values from -0.15625 to 0.15625
- conv_weight: bfloat16 [4, 2, 1536, 432], P('segment', None, 'chan'), may hold values from -0.3125 to 0.3125
- norm_gain: float32 [4, 2, 1536], P('segment', None, 'chan'), may hold values from 0.1 to 1.9
- norm_bias: float32 [4, 2, 1536], P('segment', None, 'chan'), may hold values from -4 to 4
Outputs:
- grad_latent: bfloat16 [4, 8, 1536, 256], P('segment', 'dp', None, 'chan')
- grad_proj: float32 [4, 2, 1536, 1536], P('segment', None, 'chan')
- grad_conv: float32 [4, 2, 1536, 432], P('segment', None, 'chan')
- grad_gain: float32 [4, 2, 1536], P('segment', None, 'chan')
- grad_bias: float32 [4, 2, 1536], P('segment', None, 'chan')
All inputs are finite; a program needn't handle non-finite values.
Results may differ from a plain program's by a relative error of at most 0.009.
Values may be sent and summed in bfloat16 or wider, within the bound.
No kernel may reach another device: no remote copies, remote signals or barrier semaphores. Data moves between devices by JAX's collectives and lax.ppermute only.
A program may use at most 64 MiB of HBM per device.

v0:
```python
import jax
import jax.numpy as jnp
from jax import lax
from jax.sharding import PartitionSpec as P

GS = 48
WW = 64
NORM_EPS = 1e-05


def passed_along(block, axis, distance):
    devices = range(lax.axis_size(axis))
    route = [(i - distance, i) for i in devices if i - distance in devices]
    return lax.ppermute(block, axis, route)


def shifted_cells(values, step_row, step_col, img_width):
    length = values.shape[2]
    margin = img_width + 1
    padded = jnp.pad(values, ((0, 0), (0, 0), (margin, margin)))
    start_at = margin + step_row * img_width + step_col
    part_view = lax.slice_in_dim(padded, start_at, start_at + length, axis=2)
    column = jnp.arange(length, dtype=jnp.int32) % img_width
    inside = (column + step_col >= 0) & (column + step_col < img_width)
    return jnp.where(inside, part_view, jnp.zeros((), values.dtype))


def norm_forward(saved_pre, gain_vec, bias_vec):
    chans, positions = saved_pre.shape
    groups_here = chans // GS
    pre = saved_pre.astype(jnp.float32).reshape(groups_here, GS, positions)
    centre = jnp.mean(pre, axis=(1, 2), keepdims=True)
    varied = jnp.mean(jnp.square(pre - centre), axis=(1, 2), keepdims=True)
    inv_std = lax.rsqrt(varied + NORM_EPS)
    normed = (pre - centre) * inv_std
    gain_grid = gain_vec.reshape(groups_here, GS, 1)
    scaled = normed * gain_grid + bias_vec.reshape(groups_here, GS, 1)
    gate_vals = jax.nn.sigmoid(scaled)
    act_bf = (scaled * gate_vals).astype(jnp.bfloat16).reshape(chans, positions)
    return (normed, scaled, gate_vals, inv_std, gain_grid, act_bf)


def conv_backward(grad_act, norm_state, saved_in, w_conv):
    normed, scaled, gate_vals, inv_std, gain_grid, act_bf = norm_state
    groups_here, _, positions = normed.shape
    chans = groups_here * GS
    grad_act = grad_act.reshape(groups_here, GS, positions)
    grad_norm = grad_act * (gate_vals * (1.0 + scaled * (1.0 - gate_vals)))
    gain_grad = jnp.sum(grad_norm * normed, axis=2).reshape(chans)
    bias_grad = jnp.sum(grad_norm, axis=2).reshape(chans)
    weighted = grad_norm * gain_grid
    first_mean = jnp.mean(weighted, axis=(1, 2), keepdims=True)
    second_mean = jnp.mean(weighted * normed, axis=(1, 2), keepdims=True)
    grad_pre = (inv_std * (weighted - first_mean - normed * second_mean)).astype(jnp.bfloat16)
    saved_grid = saved_in.reshape(groups_here, GS, positions)
    taps_w = w_conv.reshape(groups_here, GS, 9, GS)
    conv_parts = []
    back_sum = jnp.zeros((groups_here, GS, positions), jnp.float32)
    for tap_row in (-1, 0, 1):
        for tap_col in (-1, 0, 1):
            tap_at = 3 * (tap_row + 1) + tap_col + 1
            source = shifted_cells(saved_grid, tap_row, tap_col, WW)
            conv_parts.append(
                jnp.einsum("gop,gjp->goj", grad_pre, source, preferred_element_type=jnp.float32)
            )
            spread_back = jnp.einsum(
                "goj,gop->gjp",
                taps_w[:, :, tap_at, :],
                grad_pre,
                preferred_element_type=jnp.float32,
            )
            back_sum = back_sum + shifted_cells(spread_back, -tap_row, -tap_col, WW)
    conv_grad = jnp.stack(conv_parts, axis=2).reshape(chans, 9 * GS)
    branch = back_sum.reshape(chans, positions).astype(jnp.bfloat16)
    return (branch, conv_grad, gain_grad, bias_grad)


def block_sharded(grad_slab, saved_in, saved_pre, w_proj, w_conv, gain_vec, bias_vec):
    norm_state = norm_forward(saved_pre, gain_vec, bias_vec)
    act_bf = norm_state[5]
    grad_piece = lax.all_gather(grad_slab, "chan", axis=1, tiled=True)
    fresh = jnp.dot(w_proj, grad_piece, preferred_element_type=jnp.float32)
    weight_acc = lax.dot_general(
        act_bf, grad_piece, (((1,), (1,)), ((), ())), preferred_element_type=jnp.float32
    )
    branch, conv_grad, gain_grad, bias_grad = conv_backward(fresh, norm_state, saved_in, w_conv)
    returned = lax.all_to_all(branch, "chan", split_axis=1, concat_axis=0, tiled=True)
    out_slab = (grad_slab.astype(jnp.float32) + returned.astype(jnp.float32)).astype(jnp.bfloat16)
    return (out_slab, (weight_acc, conv_grad, gain_grad, bias_grad))


def take_micro(saved_all, index_at):
    return lax.dynamic_index_in_dim(saved_all[0], index_at, 0, keepdims=False)


def per_device(
    grad_top,
    inputs_one,
    conv_one,
    inputs_two,
    conv_two,
    proj_weight,
    conv_weight,
    norm_gain,
    norm_bias,
):
    segments = lax.axis_size("segment")
    segment_at = lax.axis_index("segment")
    local_mb = grad_top.shape[0]
    chans = conv_one.shape[2]
    width_all = proj_weight.shape[3]
    ticks = local_mb + segments - 1
    initial = (
        jnp.zeros(grad_top.shape[1:], jnp.bfloat16),
        jnp.zeros((1,) + grad_top.shape, jnp.bfloat16),
        jnp.zeros((2, chans, width_all), jnp.float32),
        jnp.zeros((2, chans, 9 * GS), jnp.float32),
        jnp.zeros((2, chans), jnp.float32),
        jnp.zeros((2, chans), jnp.float32),
    )

    def one_tick(tick_at, running):
        received, latent, proj_acc, conv_acc, gain_acc, bias_acc = running
        micro_at = tick_at - (segments - 1 - segment_at)
        is_valid = (micro_at >= 0) & (micro_at < local_mb)
        safe_mb = jnp.clip(micro_at, 0, local_mb - 1)
        top_grad = lax.dynamic_index_in_dim(grad_top, safe_mb, 0, keepdims=False)
        entering = jnp.where(segment_at == segments - 1, top_grad, received)
        mid_grad, grads_two = block_sharded(
            entering,
            take_micro(inputs_two, safe_mb),
            take_micro(conv_two, safe_mb),
            proj_weight[0, 1],
            conv_weight[0, 1],
            norm_gain[0, 1],
            norm_bias[0, 1],
        )
        out_grad, grads_one = block_sharded(
            mid_grad,
            take_micro(inputs_one, safe_mb),
            take_micro(conv_one, safe_mb),
            proj_weight[0, 0],
            conv_weight[0, 0],
            norm_gain[0, 0],
            norm_bias[0, 0],
        )
        weight_mask = is_valid.astype(jnp.float32)
        proj_acc = proj_acc + weight_mask * jnp.stack((grads_one[0], grads_two[0]))
        conv_acc = conv_acc + weight_mask * jnp.stack((grads_one[1], grads_two[1]))
        gain_acc = gain_acc + weight_mask * jnp.stack((grads_one[2], grads_two[2]))
        bias_acc = bias_acc + weight_mask * jnp.stack((grads_one[3], grads_two[3]))
        current = lax.dynamic_index_in_dim(latent[0], safe_mb, 0, keepdims=False)
        kept = jnp.where(is_valid, out_grad, current)
        latent = lax.dynamic_update_index_in_dim(latent, kept[None, None], safe_mb, 1)
        received = passed_along(out_grad, "segment", -1)
        return (received, latent, proj_acc, conv_acc, gain_acc, bias_acc)

    final = lax.fori_loop(0, ticks, one_tick, initial)
    latent = final[1]
    proj_sum, conv_sum, gain_sum, bias_sum = lax.psum(
        (final[2], final[3], final[4], final[5]), "dp"
    )
    return (latent, proj_sum[None], conv_sum[None], gain_sum[None], bias_sum[None])


def solution(mesh):
    return jax.shard_map(
        per_device,
        mesh=mesh,
        in_specs=(
            P("dp", None, "chan"),
            P("segment", "dp", "chan", None),
            P("segment", "dp", "chan", None),
            P("segment", "dp", "chan", None),
            P("segment", "dp", "chan", None),
            P("segment", None, "chan", None),
            P("segment", None, "chan", None),
            P("segment", None, "chan"),
            P("segment", None, "chan"),
        ),
        out_specs=(
            P("segment", "dp", None, "chan"),
            P("segment", None, "chan", None),
            P("segment", None, "chan", None),
            P("segment", None, "chan"),
            P("segment", None, "chan"),
        ),
        check_vma=False,
    )
```

profile of v0, /device:TPU:2, one launch (start us, length us, event | category | flops | bytes accessed | tf_op | source)
XLA Modules:
  0.0 469.4 jit_solution(2428649469921807830)
XLA Ops:
  7.3 1.8 copy.64
  9.6 357.8 %while.26 = (s32[]{:T(128)}, bf16[1536,16]{0,1:T(8,128)(2,1)S(1)}, bf16[1,1,1536,16]{2,3,1,0:T(8,128)(2,1)}, f32[2,96,1536]{2,1,0:T(8,128)S(1)}, f32[2,96,432]{1...) while((s32[]{:T(128)}, bf16[1536,16]{0,1:T(8,128)(2,1)S(1)}, ...), condition=%wide.region_21.22_spmd.clone, body=%wide.region_0.21_spmd.clone.sunk | while | flops 392720768 | bytes 27672152 | solution.py:158
  11.2 0.9 convert_reduce_fusion.5
  12.5 1.0 multiply_reduce_fusion.13
  14.7 19.7 %all_gather.24 = bf16[1536,256]{0,1:T(8,128)(2,1)S(1)} all-gather(bf16[1536,16]{0,1:T(8,128)(2,1)S(1)} %bitcast_select_fusion.3), channel_id=1, replica_groups=mesh['segment'=4,'chan'=16,'dp'=8] {'chan'}, dimensions={1}, use_global_device_ids=true | all-gather | bytes 835584 | tf_op jit(solution)/shard_map/while/body/eval_jaxpr/all_gather | solution.py:81
  34.4 2.0 multiply_reduce_fusion.14
  37.0 1.0 fusion.353
  40.7 4.4 all-to-all-start
  52.0 1.0 all-to-all-done
  53.2 18.4 %all_gather.25 = bf16[1536,256]{0,1:T(8,128)(2,1)S(1)} all-gather(bf16[1536,16]{0,1:T(8,128)(2,1)S(1)} %add_convert_fusion.4), channel_id=1, replica_groups=mesh['segment'=4,'chan'=16,'dp'=8] {'chan'}, dimensions={1}, use_global_device_ids=true | all-gather | bytes 835584 | tf_op jit(solution)/shard_map/while/body/eval_jaxpr/all_gather | solution.py:81
  71.6 2.0 multiply_reduce_fusion.15
  76.8 4.6 all-to-all-start.1
  81.5 0.8 fusion.369
  88.9 1.2 copy.167
  91.7 1.4 fusion.358
  93.2 3.9 collective-permute-start
  97.2 1.9 collective-permute-done
  100.8 0.9 convert_reduce_fusion.5
  102.1 1.0 multiply_reduce_fusion.13
  104.2 19.4 %all_gather.24 = bf16[1536,256]{0,1:T(8,128)(2,1)S(1)} all-gather(bf16[1536,16]{0,1:T(8,128)(2,1)S(1)} %bitcast_select_fusion.3), channel_id=1, replica_groups=mesh['segment'=4,'chan'=16,'dp'=8] {'chan'}, dimensions={1}, use_global_device_ids=true | all-gather | bytes 835584 | tf_op jit(solution)/shard_map/while/body/eval_jaxpr/all_gather | solution.py:81
  123.6 2.0 multiply_reduce_fusion.14
  126.2 1.0 fusion.353
  129.9 4.6 all-to-all-start
  141.4 1.0 all-to-all-done
  142.6 18.4 %all_gather.25 = bf16[1536,256]{0,1:T(8,128)(2,1)S(1)} all-gather(bf16[1536,16]{0,1:T(8,128)(2,1)S(1)} %add_convert_fusion.4), channel_id=1, replica_groups=mesh['segment'=4,'chan'=16,'dp'=8] {'chan'}, dimensions={1}, use_global_device_ids=true | all-gather | bytes 835584 | tf_op jit(solution)/shard_map/while/body/eval_jaxpr/all_gather | solution.py:81
  161.0 2.0 multiply_reduce_fusion.15
  166.3 4.6 all-to-all-start.1
  170.9 0.8 fusion.369
  178.3 1.2 copy.167
  181.2 1.4 fusion.358
  182.6 3.9 collective-permute-start
  186.6 1.9 collective-permute-done
  190.2 0.9 convert_reduce_fusion.5
  191.5 1.0 multiply_reduce_fusion.13
  193.7 19.4 %all_gather.24 = bf16[1536,256]{0,1:T(8,128)(2,1)S(1)} all-gather(bf16[1536,16]{0,1:T(8,128)(2,1)S(1)} %bitcast_select_fusion.3), channel_id=1, replica_groups=mesh['segment'=4,'chan'=16,'dp'=8] {'chan'}, dimensions={1}, use_global_device_ids=true | all-gather | bytes 835584 | tf_op jit(solution)/shard_map/while/body/eval_jaxpr/all_gather | solution.py:81
  213.1 2.0 multiply_reduce_fusion.14
  215.7 1.0 fusion.353
  219.4 4.6 all-to-all-start
  230.9 1.0 all-to-all-done
  232.1 18.4 %all_gather.25 = bf16[1536,256]{0,1:T(8,128)(2,1)S(1)} all-gather(bf16[1536,16]{0,1:T(8,128)(2,1)S(1)} %add_convert_fusion.4), channel_id=1, replica_groups=mesh['segment'=4,'chan'=16,'dp'=8] {'chan'}, dimensions={1}, use_global_device_ids=true | all-gather | bytes 835584 | tf_op jit(solution)/shard_map/while/body/eval_jaxpr/all_gather | solution.py:81
  250.5 2.0 multiply_reduce_fusion.15
  255.7 4.6 all-to-all-start.1
  267.8 1.2 copy.167
  270.6 1.4 fusion.358
  272.1 3.9 collective-permute-start
  276.1 1.9 collective-permute-done
  279.7 0.9 convert_reduce_fusion.5
  280.9 1.0 multiply_reduce_fusion.13
  283.1 19.4 %all_gather.24 = bf16[1536,256]{0,1:T(8,128)(2,1)S(1)} all-gather(bf16[1536,16]{0,1:T(8,128)(2,1)S(1)} %bitcast_select_fusion.3), channel_id=1, replica_groups=mesh['segment'=4,'chan'=16,'dp'=8] {'chan'}, dimensions={1}, use_global_device_ids=true | all-gather | bytes 835584 | tf_op jit(solution)/shard_map/while/body/eval_jaxpr/all_gather | solution.py:81
  302.5 2.0 multiply_reduce_fusion.14
  305.1 1.0 fusion.353
  308.8 4.6 all-to-all-start
  320.3 1.0 all-to-all-done
  321.5 18.4 %all_gather.25 = bf16[1536,256]{0,1:T(8,128)(2,1)S(1)} all-gather(bf16[1536,16]{0,1:T(8,128)(2,1)S(1)} %add_convert_fusion.4), channel_id=1, replica_groups=mesh['segment'=4,'chan'=16,'dp'=8] {'chan'}, dimensions={1}, use_global_device_ids=true | all-gather | bytes 835584 | tf_op jit(solution)/shard_map/while/body/eval_jaxpr/all_gather | solution.py:81
  339.9 2.0 multiply_reduce_fusion.15
  345.1 4.6 all-to-all-start.1
  357.2 1.2 copy.167
  360.0 1.4 fusion.358
  361.5 3.9 collective-permute-start
  365.5 1.9 collective-permute-done
  367.5 2.4 copy.65
  369.9 23.8 %all-reduce.18 = (f32[1,2,96]{2,1,0:T(2,128)}, f32[1,2,96]{2,1,0:T(2,128)}) all-reduce(f32[1,2,96]{2,1,0:T(2,128)S(1)} %bitcast.586, f32[1,2,96]{2,1,0:T(2,128)S(1)} %bitcast.587), channel_id=1, replica_groups=mesh['segment'=4,'chan'=16,'dp'=8] {'dp'}, use_global_device_ids=true, to_apply=%region_24.25 | all-reduce | flops 384 | bytes 3072 | tf_op jit(solution)/shard_map/psum | solution.py:160
  393.7 65.7 %all-reduce.22.cloned.1.call-done = (f32[1,2,96,1536]{3,2,1,0:T(8,128)}, f32[1,2,96,432]{3,2,1,0:T(8,128)}) async-done(((f32[1,2,96,1536]{3,2,1,0:T(8,128)}, f32[1,2,96,432]{3,2,1,0:T(8,128)}), (f32[1,2,96,1536]{3,2,1,0:T(8,128)}, f32[1,2,96,432]{3,2,1,0:T(8,128)})) %all-reduce.22.cloned.1.call-update) | async-done | bytes 1511440 | tf_op jit(solution)/shard_map/psum | solution.py:160
  459.4 2.4 copy.207
  (667 shorter events, 101.1 us)
Async XLA Ops:
  7.2 452.2 %all-reduce.22.cloned.1.call-start = ((), (), s32[]{:S(2)}) async-start(), calls=%async_computation.2 | async-start | bytes 3145728 | tf_op jit(solution)/shard_map/psum | solution.py:160
  9.7 29.8 %copy-start.30 = (pred[256]{0:T(512)(128)(4,1)}, pred[256]{0:T(512)(128)(4,1)S(1)}, u32[]{:S(2)}) copy-start(pred[256]{0:T(512)(128)(4,1)S(1)} %compare_and_fusion.7) | copy-start | bytes 772 | tf_op jit(solution)/shard_map/while
  9.7 29.8 %copy-start.27 = (pred[256]{0:T(512)(128)(4,1)}, pred[256]{0:T(512)(128)(4,1)S(1)}, u32[]{:S(2)}) copy-start(pred[256]{0:T(512)(128)(4,1)S(1)} %compare_and_fusion.8) | copy-start | bytes 772 | tf_op jit(solution)/shard_map/while
  38.8 6.3 %copy-start.2 = (bf16[1,1,96,256]{3,2,1,0:T(8,128)(2,1)S(1)}, bf16[1,1,96,256]{3,2,1,0:T(8,128)(2,1)}, u32[]{:S(2)}) copy-start(bf16[1,1,96,256]{3,2,1,0:T(8,128)(2,1)} %get-tuple-element.854) | copy-start | bytes 147460 | tf_op jit(solution)/shard_map/while
  39.5 9.8 %copy-start.7 = (bf16[1,1,96,256]{3,2,1,0:T(8,128)(2,1)S(1)}, bf16[1,1,96,256]{3,2,1,0:T(8,128)(2,1)}, u32[]{:S(2)}) copy-start(bf16[1,1,96,256]{3,2,1,0:T(8,128)(2,1)} %get-tuple-element.857) | copy-start | bytes 147460 | tf_op jit(solution)/shard_map/while
  39.8 9.5 %copy-start.31 = (pred[256]{0:T(512)(128)(4,1)S(1)}, pred[256]{0:T(512)(128)(4,1)}, u32[]{:S(2)}) copy-start(pred[256]{0:T(512)(128)(4,1)} %copy-done.30) | copy-start | bytes 772 | tf_op jit(solution)/shard_map/while
  39.8 9.9 %copy-start.28 = (pred[256]{0:T(512)(128)(4,1)S(1)}, pred[256]{0:T(512)(128)(4,1)}, u32[]{:S(2)}) copy-start(pred[256]{0:T(512)(128)(4,1)} %copy-done.27) | copy-start | bytes 772 | tf_op jit(solution)/shard_map/while
  40.7 12.3 %all-to-all-start = ((bf16[96,16,16]{0,2,1:T(8,128)(2,1)}), bf16[96,16,16]{0,2,1:T(8,128)(2,1)S(1)}, u32[]{:S(2)}, u32[]{:S(2)}) async-start(bf16[96,16,16]{0,2,1:T(8,128)(2,1)} %convert_element_type.430), calls=%async_computation | async-start | bytes 131072 | tf_op jit(solution)/shard_map/while/body/eval_jaxpr/all_to_all | solution.py:87
  52.0 19.6 %copy-start.22 = (f32[96]{0:T(128)S(1)}, f32[96]{0:T(128)}, u32[]{:S(2)}) copy-start(f32[96]{0:T(128)} %mul.953) | copy-start | bytes 1156 | tf_op jit(solution)/shard_map/while
  75.0 6.5 %copy-start.6 = (bf16[1,1,96,256]{3,2,1,0:T(8,128)(2,1)S(1)}, bf16[1,1,96,256]{3,2,1,0:T(8,128)(2,1)}, u32[]{:S(2)}) copy-start(bf16[1,1,96,256]{3,2,1,0:T(8,128)(2,1)} %get-tuple-element.856) | copy-start | bytes 147460 | tf_op jit(solution)/shard_map/while
  76.8 14.7 %all-to-all-start.1 = ((bf16[96,16,16]{0,2,1:T(8,128)(2,1)}), bf16[96,16,16]{0,2,1:T(8,128)(2,1)S(1)}, u32[]{:S(2)}, u32[]{:S(2)}) async-start(bf16[96,16,16]{0,2,1:T(8,128)(2,1)} %convert_element_type.431), calls=%async_computation.1 | async-start | bytes 131072 | tf_op jit(solution)/shard_map/while/body/eval_jaxpr/all_to_all | solution.py:87
  90.8 6.3 %copy-start.10 = (f32[2,96]{1,0:T(2,128)S(1)}, f32[2,96]{1,0:T(2,128)}, u32[]{:S(2)}) copy-start(f32[2,96]{1,0:T(2,128)} %get-tuple-element.824) | copy-start | bytes 2308 | tf_op jit(solution)/shard_map/while
  90.8 6.3 %copy-start.13 = (f32[2,96]{1,0:T(2,128)S(1)}, f32[2,96]{1,0:T(2,128)}, u32[]{:S(2)}) copy-start(f32[2,96]{1,0:T(2,128)} %get-tuple-element.825) | copy-start | bytes 2308 | tf_op jit(solution)/shard_map/while
  90.8 6.3 %copy-start.23 = (f32[96]{0:T(128)S(1)}, f32[96]{0:T(128)}, u32[]{:S(2)}) copy-start(f32[96]{0:T(128)} %get-tuple-element.792) | copy-start | bytes 1156 | tf_op jit(solution)/shard_map/while
  90.8 6.3 %copy-start.24 = (f32[96]{0:T(128)S(1)}, f32[96]{0:T(128)}, u32[]{:S(2)}) copy-start(f32[96]{0:T(128)} %get-tuple-element.794) | copy-start | bytes 1156 | tf_op jit(solution)/shard_map/while
  90.8 6.3 %copy-start.25 = (f32[96]{0:T(128)S(1)}, f32[96]{0:T(128)}, u32[]{:S(2)}) copy-start(f32[96]{0:T(128)} %get-tuple-element.793) | copy-start | bytes 1156 | tf_op jit(solution)/shard_map/while
  90.9 6.3 %copy-start.26 = (f32[96]{0:T(128)S(1)}, f32[96]{0:T(128)}, u32[]{:S(2)}) copy-start(f32[96]{0:T(128)} %get-tuple-element.795) | copy-start | bytes 1156 | tf_op jit(solution)/shard_map/while
  91.5 7.6 %copy-start.4 = (f32[2,96,432]{1,2,0:T(8,128)}, f32[2,96,432]{1,2,0:T(8,128)S(1)}, u32[]{:S(2)}) copy-start(f32[2,96,432]{1,2,0:T(8,128)S(1)} %fusion.378) | copy-start | bytes 995332 | tf_op jit(solution)/shard_map/while
  93.2 6.0 %collective-permute-start = (bf16[1536,16]{0,1:T(8,128)(2,1)S(1)}, bf16[1536,16]{0,1:T(8,128)(2,1)S(1)}, u32[]{:S(2)}, u32[]{:S(2)}) collective-permute-start(bf16[1536,16]{0,1:T(8,128)(2,1)S(1)} %get-tuple-element.790), channel_id=1, source_target_pairs={{128,0},{256,128},{384,256},{129,1},{257,129},{385,257},{130,2},{2... | collective-permute-start | bytes 147464 | tf_op jit(solution)/shard_map/while/body/eval_jaxpr/ppermute | solution.py:14
  99.2 29.5 %copy-start.30 = (pred[256]{0:T(512)(128)(4,1)}, pred[256]{0:T(512)(128)(4,1)S(1)}, u32[]{:S(2)}) copy-start(pred[256]{0:T(512)(128)(4,1)S(1)} %compare_and_fusion.7) | copy-start | bytes 772 | tf_op jit(solution)/shard_map/while
  99.2 29.5 %copy-start.27 = (pred[256]{0:T(512)(128)(4,1)}, pred[256]{0:T(512)(128)(4,1)S(1)}, u32[]{:S(2)}) copy-start(pred[256]{0:T(512)(128)(4,1)S(1)} %compare_and_fusion.8) | copy-start | bytes 772 | tf_op jit(solution)/shard_map/while
  128.0 6.5 %copy-start.2 = (bf16[1,1,96,256]{3,2,1,0:T(8,128)(2,1)S(1)}, bf16[1,1,96,256]{3,2,1,0:T(8,128)(2,1)}, u32[]{:S(2)}) copy-start(bf16[1,1,96,256]{3,2,1,0:T(8,128)(2,1)} %get-tuple-element.854) | copy-start | bytes 147460 | tf_op jit(solution)/shard_map/while
  128.7 10.0 %copy-start.7 = (bf16[1,1,96,256]{3,2,1,0:T(8,128)(2,1)S(1)}, bf16[1,1,96,256]{3,2,1,0:T(8,128)(2,1)}, u32[]{:S(2)}) copy-start(bf16[1,1,96,256]{3,2,1,0:T(8,128)(2,1)} %get-tuple-element.857) | copy-start | bytes 147460 | tf_op jit(solution)/shard_map/while
  129.0 9.7 %copy-start.31 = (pred[256]{0:T(512)(128)(4,1)S(1)}, pred[256]{0:T(512)(128)(4,1)}, u32[]{:S(2)}) copy-start(pred[256]{0:T(512)(128)(4,1)} %copy-done.30) | copy-start | bytes 772 | tf_op jit(solution)/shard_map/while
  129.0 10.1 %copy-start.28 = (pred[256]{0:T(512)(128)(4,1)S(1)}, pred[256]{0:T(512)(128)(4,1)}, u32[]{:S(2)}) copy-start(pred[256]{0:T(512)(128)(4,1)} %copy-done.27) | copy-start | bytes 772 | tf_op jit(solution)/shard_map/while
  129.9 12.5 %all-to-all-start = ((bf16[96,16,16]{0,2,1:T(8,128)(2,1)}), bf16[96,16,16]{0,2,1:T(8,128)(2,1)S(1)}, u32[]{:S(2)}, u32[]{:S(2)}) async-start(bf16[96,16,16]{0,2,1:T(8,128)(2,1)} %convert_element_type.430), calls=%async_computation | async-start | bytes 131072 | tf_op jit(solution)/shard_map/while/body/eval_jaxpr/all_to_all | solution.py:87
  141.4 19.6 %copy-start.22 = (f32[96]{0:T(128)S(1)}, f32[96]{0:T(128)}, u32[]{:S(2)}) copy-start(f32[96]{0:T(128)} %mul.953) | copy-start | bytes 1156 | tf_op jit(solution)/shard_map/while
  164.4 6.5 %copy-start.6 = (bf16[1,1,96,256]{3,2,1,0:T(8,128)(2,1)S(1)}, bf16[1,1,96,256]{3,2,1,0:T(8,128)(2,1)}, u32[]{:S(2)}) copy-start(bf16[1,1,96,256]{3,2,1,0:T(8,128)(2,1)} %get-tuple-element.856) | copy-start | bytes 147460 | tf_op jit(solution)/shard_map/while
  166.3 14.7 %all-to-all-start.1 = ((bf16[96,16,16]{0,2,1:T(8,128)(2,1)}), bf16[96,16,16]{0,2,1:T(8,128)(2,1)S(1)}, u32[]{:S(2)}, u32[]{:S(2)}) async-start(bf16[96,16,16]{0,2,1:T(8,128)(2,1)} %convert_element_type.431), calls=%async_computation.1 | async-start | bytes 131072 | tf_op jit(solution)/shard_map/while/body/eval_jaxpr/all_to_all | solution.py:87
  180.2 6.3 %copy-start.10 = (f32[2,96]{1,0:T(2,128)S(1)}, f32[2,96]{1,0:T(2,128)}, u32[]{:S(2)}) copy-start(f32[2,96]{1,0:T(2,128)} %get-tuple-element.824) | copy-start | bytes 2308 | tf_op jit(solution)/shard_map/while
  180.2 6.3 %copy-start.13 = (f32[2,96]{1,0:T(2,128)S(1)}, f32[2,96]{1,0:T(2,128)}, u32[]{:S(2)}) copy-start(f32[2,96]{1,0:T(2,128)} %get-tuple-element.825) | copy-start | bytes 2308 | tf_op jit(solution)/shard_map/while
  180.3 6.3 %copy-start.23 = (f32[96]{0:T(128)S(1)}, f32[96]{0:T(128)}, u32[]{:S(2)}) copy-start(f32[96]{0:T(128)} %get-tuple-element.792) | copy-start | bytes 1156 | tf_op jit(solution)/shard_map/while
  180.3 6.3 %copy-start.24 = (f32[96]{0:T(128)S(1)}, f32[96]{0:T(128)}, u32[]{:S(2)}) copy-start(f32[96]{0:T(128)} %get-tuple-element.794) | copy-start | bytes 1156 | tf_op jit(solution)/shard_map/while
  180.3 6.3 %copy-start.25 = (f32[96]{0:T(128)S(1)}, f32[96]{0:T(128)}, u32[]{:S(2)}) copy-start(f32[96]{0:T(128)} %get-tuple-element.793) | copy-start | bytes 1156 | tf_op jit(solution)/shard_map/while
  181.0 7.6 %copy-start.4 = (f32[2,96,432]{1,2,0:T(8,128)}, f32[2,96,432]{1,2,0:T(8,128)S(1)}, u32[]{:S(2)}) copy-start(f32[2,96,432]{1,2,0:T(8,128)S(1)} %fusion.378) | copy-start | bytes 995332 | tf_op jit(solution)/shard_map/while
  182.6 6.0 %collective-permute-start = (bf16[1536,16]{0,1:T(8,128)(2,1)S(1)}, bf16[1536,16]{0,1:T(8,128)(2,1)S(1)}, u32[]{:S(2)}, u32[]{:S(2)}) collective-permute-start(bf16[1536,16]{0,1:T(8,128)(2,1)S(1)} %get-tuple-element.790), channel_id=1, source_target_pairs={{128,0},{256,128},{384,256},{129,1},{257,129},{385,257},{130,2},{2... | collective-permute-start | bytes 147464 | tf_op jit(solution)/shard_map/while/body/eval_jaxpr/ppermute | solution.py:14
  188.6 29.5 %copy-start.30 = (pred[256]{0:T(512)(128)(4,1)}, pred[256]{0:T(512)(128)(4,1)S(1)}, u32[]{:S(2)}) copy-start(pred[256]{0:T(512)(128)(4,1)S(1)} %compare_and_fusion.7) | copy-start | bytes 772 | tf_op jit(solution)/shard_map/while
  188.7 29.5 %copy-start.27 = (pred[256]{0:T(512)(128)(4,1)}, pred[256]{0:T(512)(128)(4,1)S(1)}, u32[]{:S(2)}) copy-start(pred[256]{0:T(512)(128)(4,1)S(1)} %compare_and_fusion.8) | copy-start | bytes 772 | tf_op jit(solution)/shard_map/while
  217.5 6.5 %copy-start.2 = (bf16[1,1,96,256]{3,2,1,0:T(8,128)(2,1)S(1)}, bf16[1,1,96,256]{3,2,1,0:T(8,128)(2,1)}, u32[]{:S(2)}) copy-start(bf16[1,1,96,256]{3,2,1,0:T(8,128)(2,1)} %get-tuple-element.854) | copy-start | bytes 147460 | tf_op jit(solution)/shard_map/while
  218.2 10.0 %copy-start.7 = (bf16[1,1,96,256]{3,2,1,0:T(8,128)(2,1)S(1)}, bf16[1,1,96,256]{3,2,1,0:T(8,128)(2,1)}, u32[]{:S(2)}) copy-start(bf16[1,1,96,256]{3,2,1,0:T(8,128)(2,1)} %get-tuple-element.857) | copy-start | bytes 147460 | tf_op jit(solution)/shard_map/while
  218.5 9.7 %copy-start.31 = (pred[256]{0:T(512)(128)(4,1)S(1)}, pred[256]{0:T(512)(128)(4,1)}, u32[]{:S(2)}) copy-start(pred[256]{0:T(512)(128)(4,1)} %copy-done.30) | copy-start | bytes 772 | tf_op jit(solution)/shard_map/while
  218.5 10.1 %copy-start.28 = (pred[256]{0:T(512)(128)(4,1)S(1)}, pred[256]{0:T(512)(128)(4,1)}, u32[]{:S(2)}) copy-start(pred[256]{0:T(512)(128)(4,1)} %copy-done.27) | copy-start | bytes 772 | tf_op jit(solution)/shard_map/while
  219.4 12.5 %all-to-all-start = ((bf16[96,16,16]{0,2,1:T(8,128)(2,1)}), bf16[96,16,16]{0,2,1:T(8,128)(2,1)S(1)}, u32[]{:S(2)}, u32[]{:S(2)}) async-start(bf16[96,16,16]{0,2,1:T(8,128)(2,1)} %convert_element_type.430), calls=%async_computation | async-start | bytes 131072 | tf_op jit(solution)/shard_map/while/body/eval_jaxpr/all_to_all | solution.py:87
  230.9 19.6 %copy-start.22 = (f32[96]{0:T(128)S(1)}, f32[96]{0:T(128)}, u32[]{:S(2)}) copy-start(f32[96]{0:T(128)} %mul.953) | copy-start | bytes 1156 | tf_op jit(solution)/shard_map/while
  253.8 6.5 %copy-start.6 = (bf16[1,1,96,256]{3,2,1,0:T(8,128)(2,1)S(1)}, bf16[1,1,96,256]{3,2,1,0:T(8,128)(2,1)}, u32[]{:S(2)}) copy-start(bf16[1,1,96,256]{3,2,1,0:T(8,128)(2,1)} %get-tuple-element.856) | copy-start | bytes 147460 | tf_op jit(solution)/shard_map/while
  255.7 14.7 %all-to-all-start.1 = ((bf16[96,16,16]{0,2,1:T(8,128)(2,1)}), bf16[96,16,16]{0,2,1:T(8,128)(2,1)S(1)}, u32[]{:S(2)}, u32[]{:S(2)}) async-start(bf16[96,16,16]{0,2,1:T(8,128)(2,1)} %convert_element_type.431), calls=%async_computation.1 | async-start | bytes 131072 | tf_op jit(solution)/shard_map/while/body/eval_jaxpr/all_to_all | solution.py:87
  269.7 6.3 %copy-start.10 = (f32[2,96]{1,0:T(2,128)S(1)}, f32[2,96]{1,0:T(2,128)}, u32[]{:S(2)}) copy-start(f32[2,96]{1,0:T(2,128)} %get-tuple-element.824) | copy-start | bytes 2308 | tf_op jit(solution)/shard_map/while
  269.7 6.3 %copy-start.13 = (f32[2,96]{1,0:T(2,128)S(1)}, f32[2,96]{1,0:T(2,128)}, u32[]{:S(2)}) copy-start(f32[2,96]{1,0:T(2,128)} %get-tuple-element.825) | copy-start | bytes 2308 | tf_op jit(solution)/shard_map/while
  270.4 7.6 %copy-start.4 = (f32[2,96,432]{1,2,0:T(8,128)}, f32[2,96,432]{1,2,0:T(8,128)S(1)}, u32[]{:S(2)}) copy-start(f32[2,96,432]{1,2,0:T(8,128)S(1)} %fusion.378) | copy-start | bytes 995332 | tf_op jit(solution)/shard_map/while
  272.1 6.0 %collective-permute-start = (bf16[1536,16]{0,1:T(8,128)(2,1)S(1)}, bf16[1536,16]{0,1:T(8,128)(2,1)S(1)}, u32[]{:S(2)}, u32[]{:S(2)}) collective-permute-start(bf16[1536,16]{0,1:T(8,128)(2,1)S(1)} %get-tuple-element.790), channel_id=1, source_target_pairs={{128,0},{256,128},{384,256},{129,1},{257,129},{385,257},{130,2},{2... | collective-permute-start | bytes 147464 | tf_op jit(solution)/shard_map/while/body/eval_jaxpr/ppermute | solution.py:14
  278.1 29.5 %copy-start.30 = (pred[256]{0:T(512)(128)(4,1)}, pred[256]{0:T(512)(128)(4,1)S(1)}, u32[]{:S(2)}) copy-start(pred[256]{0:T(512)(128)(4,1)S(1)} %compare_and_fusion.7) | copy-start | bytes 772 | tf_op jit(solution)/shard_map/while
  278.1 29.5 %copy-start.27 = (pred[256]{0:T(512)(128)(4,1)}, pred[256]{0:T(512)(128)(4,1)S(1)}, u32[]{:S(2)}) copy-start(pred[256]{0:T(512)(128)(4,1)S(1)} %compare_and_fusion.8) | copy-start | bytes 772 | tf_op jit(solution)/shard_map/while
  306.9 6.5 %copy-start.2 = (bf16[1,1,96,256]{3,2,1,0:T(8,128)(2,1)S(1)}, bf16[1,1,96,256]{3,2,1,0:T(8,128)(2,1)}, u32[]{:S(2)}) copy-start(bf16[1,1,96,256]{3,2,1,0:T(8,128)(2,1)} %get-tuple-element.854) | copy-start | bytes 147460 | tf_op jit(solution)/shard_map/while
  307.6 10.0 %copy-start.7 = (bf16[1,1,96,256]{3,2,1,0:T(8,128)(2,1)S(1)}, bf16[1,1,96,256]{3,2,1,0:T(8,128)(2,1)}, u32[]{:S(2)}) copy-start(bf16[1,1,96,256]{3,2,1,0:T(8,128)(2,1)} %get-tuple-element.857) | copy-start | bytes 147460 | tf_op jit(solution)/shard_map/while
  307.9 9.7 %copy-start.31 = (pred[256]{0:T(512)(128)(4,1)S(1)}, pred[256]{0:T(512)(128)(4,1)}, u32[]{:S(2)}) copy-start(pred[256]{0:T(512)(128)(4,1)} %copy-done.30) | copy-start | bytes 772 | tf_op jit(solution)/shard_map/while
  307.9 10.1 %copy-start.28 = (pred[256]{0:T(512)(128)(4,1)S(1)}, pred[256]{0:T(512)(128)(4,1)}, u32[]{:S(2)}) copy-start(pred[256]{0:T(512)(128)(4,1)} %copy-done.27) | copy-start | bytes 772 | tf_op jit(solution)/shard_map/while
  308.8 12.5 %all-to-all-start = ((bf16[96,16,16]{0,2,1:T(8,128)(2,1)}), bf16[96,16,16]{0,2,1:T(8,128)(2,1)S(1)}, u32[]{:S(2)}, u32[]{:S(2)}) async-start(bf16[96,16,16]{0,2,1:T(8,128)(2,1)} %convert_element_type.430), calls=%async_computation | async-start | bytes 131072 | tf_op jit(solution)/shard_map/while/body/eval_jaxpr/all_to_all | solution.py:87
  320.3 19.6 %copy-start.22 = (f32[96]{0:T(128)S(1)}, f32[96]{0:T(128)}, u32[]{:S(2)}) copy-start(f32[96]{0:T(128)} %mul.953) | copy-start | bytes 1156 | tf_op jit(solution)/shard_map/while
  343.3 6.5 %copy-start.6 = (bf16[1,1,96,256]{3,2,1,0:T(8,128)(2,1)S(1)}, bf16[1,1,96,256]{3,2,1,0:T(8,128)(2,1)}, u32[]{:S(2)}) copy-start(bf16[1,1,96,256]{3,2,1,0:T(8,128)(2,1)} %get-tuple-element.856) | copy-start | bytes 147460 | tf_op jit(solution)/shard_map/while
  345.1 14.7 %all-to-all-start.1 = ((bf16[96,16,16]{0,2,1:T(8,128)(2,1)}), bf16[96,16,16]{0,2,1:T(8,128)(2,1)S(1)}, u32[]{:S(2)}, u32[]{:S(2)}) async-start(bf16[96,16,16]{0,2,1:T(8,128)(2,1)} %convert_element_type.431), calls=%async_computation.1 | async-start | bytes 131072 | tf_op jit(solution)/shard_map/while/body/eval_jaxpr/all_to_all | solution.py:87
  359.1 6.3 %copy-start.10 = (f32[2,96]{1,0:T(2,128)S(1)}, f32[2,96]{1,0:T(2,128)}, u32[]{:S(2)}) copy-start(f32[2,96]{1,0:T(2,128)} %get-tuple-element.824) | copy-start | bytes 2308 | tf_op jit(solution)/shard_map/while
  359.1 6.3 %copy-start.13 = (f32[2,96]{1,0:T(2,128)S(1)}, f32[2,96]{1,0:T(2,128)}, u32[]{:S(2)}) copy-start(f32[2,96]{1,0:T(2,128)} %get-tuple-element.825) | copy-start | bytes 2308 | tf_op jit(solution)/shard_map/while
  359.8 7.6 %copy-start.4 = (f32[2,96,432]{1,2,0:T(8,128)}, f32[2,96,432]{1,2,0:T(8,128)S(1)}, u32[]{:S(2)}) copy-start(f32[2,96,432]{1,2,0:T(8,128)S(1)} %fusion.378) | copy-start | bytes 995332 | tf_op jit(solution)/shard_map/while
  361.5 6.0 %collective-permute-start = (bf16[1536,16]{0,1:T(8,128)(2,1)S(1)}, bf16[1536,16]{0,1:T(8,128)(2,1)S(1)}, u32[]{:S(2)}, u32[]{:S(2)}) collective-permute-start(bf16[1536,16]{0,1:T(8,128)(2,1)S(1)} %get-tuple-element.790), channel_id=1, source_target_pairs={{128,0},{256,128},{384,256},{129,1},{257,129},{385,257},{130,2},{2... | collective-permute-start | bytes 147464 | tf_op jit(solution)/shard_map/while/body/eval_jaxpr/ppermute | solution.py:14
  (69 other events, 161.8 us)
Sparse Core Ops, SparseCore 0:
  370.0 89.2 all-reduce.21
where the time goes:
time: 472 us; the launch traced here: 469 us
  blocking collectives  175 us (37%)
  waiting for transfers between devices  77.5 us (16%)
  matrix products  66.1 us (14%)
  local copies, waits for them, and re-layouts  56 us (12%)
  starting transfers between devices  52.6 us (11%)
  other arithmetic  25.2 us (5%)
  between operations  14.1 us (3%)
    all_gather x8, blocking collectives, block_sharded(): grad_piece = lax.all_gather(grad_slab, 'chan', axis=1, tiled=True)  152 us
    psum x1, waiting for transfers between devices, per_device(): lax.psum((final[2], final[3], final[4], final[5]), 'dp')  65.7 us
    dot_general x72, matrix products, conv_backward(): jnp.einsum('gop,gjp->goj', grad_pre, source, preferred_element_type=jnp.f...  36.9 us
    all_to_all x8, starting transfers between devices, block_sharded(): lax.all_to_all(branch, 'chan', split_axis=1, concat_axis=0, tiled=True)  36.9 us
    psum x1, blocking collectives, per_device(): lax.psum((final[2], final[3], final[4], final[5]), 'dp')  23.8 us
    dot_general x8, matrix products, block_sharded(): fresh = jnp.dot(w_proj, grad_piece, preferred_element_type=jnp.float32)  16 us
    ppermute x4, starting transfers between devices, passed_along(): return lax.ppermute(block, axis, route)  15.7 us
    dot_general x72, matrix products, conv_backward(): jnp.einsum('goj,gop->gjp', taps_w[:, :, tap_at, :], grad_pre, preferred_e...  10.6 us
  transfers between devices with their start and end apart: 13, of which 9 were waited for; matrix products, arithmetic and copies ran while one was open for 13% of the time, Pallas kernels for 0%

commit v1 on v0

--- a/solution.py
+++ b/solution.py
@@ -84,7 +84,10 @@
         act_bf, grad_piece, (((1,), (1,)), ((), ())), preferred_element_type=jnp.float32
     )
     branch, conv_grad, gain_grad, bias_grad = conv_backward(fresh, norm_state, saved_in, w_conv)
-    returned = lax.all_to_all(branch, "chan", split_axis=1, concat_axis=0, tiled=True)
+    returned = jnp.concatenate(
+        lax.all_to_all(jnp.stack(jnp.split(branch, lax.axis_size("chan"), axis=1)), "chan", 0, 0),
+        axis=0,
+    )
     out_slab = (grad_slab.astype(jnp.float32) + returned.astype(jnp.float32)).astype(jnp.bfloat16)
     return (out_slab, (weight_acc, conv_grad, gain_grad, bias_grad))
 

time: 472 us -> 553 us (1.17)
  local copies, waits for them, and re-layouts: 56 us -> 137 us
    while x232 -> x480, local copies, waits for them, and re-layouts: 4.38 us -> 86.2 us
    convert_element_type x16 -> x0, local copies, waits for them, and re-layouts: 6.92 us -> none  [conv_backward(): branch = back_sum.reshape(chans, positions).astype(jnp.bfloat16)]
  transfers between devices with their start and end apart: 13 -> 13, of which waited for: 9 -> 9; matrix products, arithmetic and copies ran while one was open for 13% -> 11% of each run, Pallas kernels for 0% -> 0%
where the time goes in v1:
time: 553 us; the launch traced here: 551 us
  blocking collectives  176 us (32%)
  local copies, waits for them, and re-layouts  137 us (25%)
  waiting for transfers between devices  77.2 us (14%)
  matrix products  66.4 us (12%)
  starting transfers between devices  52.6 us (10%)
  other arithmetic  25.1 us (5%)
  between operations  14.1 us (3%)
    all_gather x8, blocking collectives, block_sharded(): grad_piece = lax.all_gather(grad_slab, 'chan', axis=1, tiled=True)  152 us
    while x480, local copies, waits for them, and re-layouts  86.2 us
    psum x1, waiting for transfers between devices, per_device(): lax.psum((final[2], final[3], final[4], final[5]), 'dp')  65.7 us
    dot_general x72, matrix products, conv_backward(): jnp.einsum('gop,gjp->goj', grad_pre, source, preferred_element_type=jnp.f...  36.9 us
    all_to_all x8, starting transfers between devices, block_sharded(): lax.all_to_all(jnp.stack(jnp.split(branch, lax.axis_size('chan'), axis=1)...  36.9 us
    psum x1, blocking collectives, per_device(): lax.psum((final[2], final[3], final[4], final[5]), 'dp')  23.8 us
    dot_general x8, matrix products, block_sharded(): fresh = jnp.dot(w_proj, grad_piece, preferred_element_type=jnp.float32)  16.2 us
    ppermute x4, starting transfers between devices, passed_along(): return lax.ppermute(block, axis, route)  15.7 us
  transfers between devices with their start and end apart: 13, of which 9 were waited for; matrix products, arithmetic and copies ran while one was open for 11% of the time, Pallas kernels for 0%

profile of v1, /device:TPU:2, one launch (start us, length us, event | category | flops | bytes accessed | tf_op | source)
XLA Modules:
  0.0 550.8 jit_solution(8605253235901828258)
XLA Ops:
  7.3 1.8 copy.94
  9.6 439.2 %while.26 = (s32[]{:T(128)}, bf16[1536,16]{0,1:T(8,128)(2,1)S(1)}, bf16[1,1,1536,16]{2,3,1,0:T(8,128)(2,1)}, f32[2,96,1536]{2,1,0:T(8,128)S(1)}, f32[2,96,432]{1...) while((s32[]{:T(128)}, bf16[1536,16]{0,1:T(8,128)(2,1)S(1)}, ...), condition=%wide.region_21.22_spmd.clone, body=%wide.region_0.21_spmd.clone.sunk | while | flops 392671616 | bytes 27508312 | solution.py:161
  11.2 0.9 convert_reduce_fusion.5
  12.5 1.0 multiply_reduce_fusion.13
  14.7 19.7 %all_gather.24 = bf16[1536,256]{0,1:T(8,128)(2,1)S(1)} all-gather(bf16[1536,16]{0,1:T(8,128)(2,1)S(1)} %bitcast_select_fusion.3), channel_id=1, replica_groups=mesh['segment'=4,'chan'=16,'dp'=8] {'chan'}, dimensions={1}, use_global_device_ids=true | all-gather | bytes 835584 | tf_op jit(solution)/shard_map/while/body/eval_jaxpr/all_gather | solution.py:81
  34.4 2.0 multiply_reduce_fusion.14
  37.0 1.0 fusion.357
  50.9 4.4 all-to-all-start
  62.2 0.9 all-to-all-done
  63.3 18.5 %all_gather.25 = bf16[1536,256]{0,1:T(8,128)(2,1)S(1)} all-gather(bf16[1536,16]{0,1:T(8,128)(2,1)S(1)} %add_convert_fusion.4), channel_id=1, replica_groups=mesh['segment'=4,'chan'=16,'dp'=8] {'chan'}, dimensions={1}, use_global_device_ids=true | all-gather | bytes 835584 | tf_op jit(solution)/shard_map/while/body/eval_jaxpr/all_gather | solution.py:81
  81.8 2.0 multiply_reduce_fusion.15
  97.2 4.6 all-to-all-start.1
  101.9 0.8 fusion.375
  109.3 1.2 copy.289
  112.1 1.5 fusion.364
  113.5 3.9 collective-permute-start
  117.6 1.9 collective-permute-done
  121.1 0.9 convert_reduce_fusion.5
  122.4 1.0 multiply_reduce_fusion.13
  124.6 19.4 %all_gather.24 = bf16[1536,256]{0,1:T(8,128)(2,1)S(1)} all-gather(bf16[1536,16]{0,1:T(8,128)(2,1)S(1)} %bitcast_select_fusion.3), channel_id=1, replica_groups=mesh['segment'=4,'chan'=16,'dp'=8] {'chan'}, dimensions={1}, use_global_device_ids=true | all-gather | bytes 835584 | tf_op jit(solution)/shard_map/while/body/eval_jaxpr/all_gather | solution.py:81
  144.0 2.0 multiply_reduce_fusion.14
  146.6 1.0 fusion.357
  160.4 4.6 all-to-all-start
  172.0 0.9 all-to-all-done
  173.1 18.5 %all_gather.25 = bf16[1536,256]{0,1:T(8,128)(2,1)S(1)} all-gather(bf16[1536,16]{0,1:T(8,128)(2,1)S(1)} %add_convert_fusion.4), channel_id=1, replica_groups=mesh['segment'=4,'chan'=16,'dp'=8] {'chan'}, dimensions={1}, use_global_device_ids=true | all-gather | bytes 835584 | tf_op jit(solution)/shard_map/while/body/eval_jaxpr/all_gather | solution.py:81
  191.6 2.0 multiply_reduce_fusion.15
  207.0 4.6 all-to-all-start.1
  211.6 0.8 fusion.375
  219.1 1.2 copy.289
  221.9 1.5 fusion.364
  223.3 3.9 collective-permute-start
  227.3 1.9 collective-permute-done
  230.9 0.9 convert_reduce_fusion.5
  232.2 1.0 multiply_reduce_fusion.13
  234.4 19.4 %all_gather.24 = bf16[1536,256]{0,1:T(8,128)(2,1)S(1)} all-gather(bf16[1536,16]{0,1:T(8,128)(2,1)S(1)} %bitcast_select_fusion.3), channel_id=1, replica_groups=mesh['segment'=4,'chan'=16,'dp'=8] {'chan'}, dimensions={1}, use_global_device_ids=true | all-gather | bytes 835584 | tf_op jit(solution)/shard_map/while/body/eval_jaxpr/all_gather | solution.py:81
  253.8 2.0 multiply_reduce_fusion.14
  256.4 1.0 fusion.357
  270.2 4.6 all-to-all-start
  281.8 0.9 all-to-all-done
  282.9 18.5 %all_gather.25 = bf16[1536,256]{0,1:T(8,128)(2,1)S(1)} all-gather(bf16[1536,16]{0,1:T(8,128)(2,1)S(1)} %add_convert_fusion.4), channel_id=1, replica_groups=mesh['segment'=4,'chan'=16,'dp'=8] {'chan'}, dimensions={1}, use_global_device_ids=true | all-gather | bytes 835584 | tf_op jit(solution)/shard_map/while/body/eval_jaxpr/all_gather | solution.py:81
  301.4 2.0 multiply_reduce_fusion.15
  316.8 4.6 all-to-all-start.1
  328.9 1.2 copy.289
  331.6 1.5 fusion.364
  333.1 3.9 collective-permute-start
  337.1 1.9 collective-permute-done
  340.7 0.9 convert_reduce_fusion.5
  342.0 1.0 multiply_reduce_fusion.13
  344.2 19.4 %all_gather.24 = bf16[1536,256]{0,1:T(8,128)(2,1)S(1)} all-gather(bf16[1536,16]{0,1:T(8,128)(2,1)S(1)} %bitcast_select_fusion.3), channel_id=1, replica_groups=mesh['segment'=4,'chan'=16,'dp'=8] {'chan'}, dimensions={1}, use_global_device_ids=true | all-gather | bytes 835584 | tf_op jit(solution)/shard_map/while/body/eval_jaxpr/all_gather | solution.py:81
  363.6 2.0 multiply_reduce_fusion.14
  366.1 1.0 fusion.357
  380.0 4.6 all-to-all-start
  391.6 0.9 all-to-all-done
  392.7 18.5 %all_gather.25 = bf16[1536,256]{0,1:T(8,128)(2,1)S(1)} all-gather(bf16[1536,16]{0,1:T(8,128)(2,1)S(1)} %add_convert_fusion.4), channel_id=1, replica_groups=mesh['segment'=4,'chan'=16,'dp'=8] {'chan'}, dimensions={1}, use_global_device_ids=true | all-gather | bytes 835584 | tf_op jit(solution)/shard_map/while/body/eval_jaxpr/all_gather | solution.py:81
  411.2 2.0 multiply_reduce_fusion.15
  426.6 4.6 all-to-all-start.1
  438.6 1.2 copy.289
  441.4 1.5 fusion.364
  442.9 3.9 collective-permute-start
  446.9 1.9 collective-permute-done
  448.9 2.4 copy.95
  451.3 23.8 %all-reduce.18 = (f32[1,2,96]{2,1,0:T(2,128)}, f32[1,2,96]{2,1,0:T(2,128)}) all-reduce(f32[1,2,96]{2,1,0:T(2,128)S(1)} %bitcast.710, f32[1,2,96]{2,1,0:T(2,128)S(1)} %bitcast.711), channel_id=1, replica_groups=mesh['segment'=4,'chan'=16,'dp'=8] {'dp'}, use_global_device_ids=true, to_apply=%region_24.25 | all-reduce | flops 384 | bytes 3072 | tf_op jit(solution)/shard_map/psum | solution.py:163
  475.1 65.7 %all-reduce.22.cloned.1.call-done = (f32[1,2,96,1536]{3,2,1,0:T(8,128)}, f32[1,2,96,432]{3,2,1,0:T(8,128)}) async-done(((f32[1,2,96,1536]{3,2,1,0:T(8,128)}, f32[1,2,96,432]{3,2,1,0:T(8,128)}), (f32[1,2,96,1536]{3,2,1,0:T(8,128)}, f32[1,2,96,432]{3,2,1,0:T(8,128)})) %all-reduce.22.cloned.1.call-update) | async-done | bytes 1511440 | tf_op jit(solution)/shard_map/psum | solution.py:163
  540.8 2.4 copy.359
  (907 shorter events, 182.1 us)
Async XLA Ops:
  7.2 533.6 %all-reduce.22.cloned.1.call-start = ((), (), s32[]{:S(2)}) async-start(), calls=%async_computation.2 | async-start | bytes 3145728 | tf_op jit(solution)/shard_map/psum | solution.py:163
  9.7 29.8 %copy-start.30 = (pred[256]{0:T(512)(128)(4,1)}, pred[256]{0:T(512)(128)(4,1)S(1)}, u32[]{:S(2)}) copy-start(pred[256]{0:T(512)(128)(4,1)S(1)} %compare_and_fusion.7) | copy-start | bytes 772 | tf_op jit(solution)/shard_map/while
  9.7 29.8 %copy-start.27 = (pred[256]{0:T(512)(128)(4,1)}, pred[256]{0:T(512)(128)(4,1)S(1)}, u32[]{:S(2)}) copy-start(pred[256]{0:T(512)(128)(4,1)S(1)} %compare_and_fusion.8) | copy-start | bytes 772 | tf_op jit(solution)/shard_map/while
  39.5 15.8 %copy-start.2 = (bf16[1,1,96,256]{3,2,1,0:T(8,128)(2,1)S(1)}, bf16[1,1,96,256]{3,2,1,0:T(8,128)(2,1)}, u32[]{:S(2)}) copy-start(bf16[1,1,96,256]{3,2,1,0:T(8,128)(2,1)} %get-tuple-element.978) | copy-start | bytes 147460 | tf_op jit(solution)/shard_map/while
  39.8 19.7 %copy-start.7 = (bf16[1,1,96,256]{3,2,1,0:T(8,128)(2,1)S(1)}, bf16[1,1,96,256]{3,2,1,0:T(8,128)(2,1)}, u32[]{:S(2)}) copy-start(bf16[1,1,96,256]{3,2,1,0:T(8,128)(2,1)} %get-tuple-element.981) | copy-start | bytes 147460 | tf_op jit(solution)/shard_map/while
  39.8 19.7 %copy-start.31 = (pred[256]{0:T(512)(128)(4,1)S(1)}, pred[256]{0:T(512)(128)(4,1)}, u32[]{:S(2)}) copy-start(pred[256]{0:T(512)(128)(4,1)} %copy-done.30) | copy-start | bytes 772 | tf_op jit(solution)/shard_map/while
  40.0 20.0 %copy-start.28 = (pred[256]{0:T(512)(128)(4,1)S(1)}, pred[256]{0:T(512)(128)(4,1)}, u32[]{:S(2)}) copy-start(pred[256]{0:T(512)(128)(4,1)} %copy-done.27) | copy-start | bytes 772 | tf_op jit(solution)/shard_map/while
  50.9 12.3 %all-to-all-start = ((bf16[16,96,16]{1,2,0:T(8,128)(2,1)}), bf16[16,96,16]{1,2,0:T(8,128)(2,1)S(1)}, u32[]{:S(2)}, u32[]{:S(2)}) async-start(bf16[16,96,16]{1,2,0:T(8,128)(2,1)} %constant_dynamic-update-slice_fusion.79), calls=%async_computation | async-start | bytes 131072 | tf_op jit(solution)/shard_map/while/body/eval_jaxpr/all_to_all | solution.py:88
  61.9 19.9 %copy-start.22 = (f32[96]{0:T(128)S(1)}, f32[96]{0:T(128)}, u32[]{:S(2)}) copy-start(f32[96]{0:T(128)} %mul.953) | copy-start | bytes 1156 | tf_op jit(solution)/shard_map/while
  85.9 15.9 %copy-start.6 = (bf16[1,1,96,256]{3,2,1,0:T(8,128)(2,1)S(1)}, bf16[1,1,96,256]{3,2,1,0:T(8,128)(2,1)}, u32[]{:S(2)}) copy-start(bf16[1,1,96,256]{3,2,1,0:T(8,128)(2,1)} %get-tuple-element.980) | copy-start | bytes 147460 | tf_op jit(solution)/shard_map/while
  97.2 14.7 %all-to-all-start.1 = ((bf16[16,96,16]{1,2,0:T(8,128)(2,1)}), bf16[16,96,16]{1,2,0:T(8,128)(2,1)S(1)}, u32[]{:S(2)}, u32[]{:S(2)}) async-start(bf16[16,96,16]{1,2,0:T(8,128)(2,1)} %constant_dynamic-update-slice_fusion.95), calls=%async_computation.1 | async-start | bytes 131072 | tf_op jit(solution)/shard_map/while/body/eval_jaxpr/all_to_all | solution.py:88
  111.2 6.3 %copy-start.10 = (f32[2,96]{1,0:T(2,128)S(1)}, f32[2,96]{1,0:T(2,128)}, u32[]{:S(2)}) copy-start(f32[2,96]{1,0:T(2,128)} %get-tuple-element.948) | copy-start | bytes 2308 | tf_op jit(solution)/shard_map/while
  111.2 6.3 %copy-start.13 = (f32[2,96]{1,0:T(2,128)S(1)}, f32[2,96]{1,0:T(2,128)}, u32[]{:S(2)}) copy-start(f32[2,96]{1,0:T(2,128)} %get-tuple-element.949) | copy-start | bytes 2308 | tf_op jit(solution)/shard_map/while
  111.2 6.3 %copy-start.23 = (f32[96]{0:T(128)S(1)}, f32[96]{0:T(128)}, u32[]{:S(2)}) copy-start(f32[96]{0:T(128)} %get-tuple-element.916) | copy-start | bytes 1156 | tf_op jit(solution)/shard_map/while
  111.2 6.3 %copy-start.24 = (f32[96]{0:T(128)S(1)}, f32[96]{0:T(128)}, u32[]{:S(2)}) copy-start(f32[96]{0:T(128)} %get-tuple-element.918) | copy-start | bytes 1156 | tf_op jit(solution)/shard_map/while
  111.2 6.3 %copy-start.25 = (f32[96]{0:T(128)S(1)}, f32[96]{0:T(128)}, u32[]{:S(2)}) copy-start(f32[96]{0:T(128)} %get-tuple-element.917) | copy-start | bytes 1156 | tf_op jit(solution)/shard_map/while
  111.2 6.3 %copy-start.26 = (f32[96]{0:T(128)S(1)}, f32[96]{0:T(128)}, u32[]{:S(2)}) copy-start(f32[96]{0:T(128)} %get-tuple-element.919) | copy-start | bytes 1156 | tf_op jit(solution)/shard_map/while
  111.9 7.6 %copy-start.4 = (f32[2,96,432]{1,2,0:T(8,128)}, f32[2,96,432]{1,2,0:T(8,128)S(1)}, u32[]{:S(2)}) copy-start(f32[2,96,432]{1,2,0:T(8,128)S(1)} %fusion.384) | copy-start | bytes 995332 | tf_op jit(solution)/shard_map/while
  113.5 6.0 %collective-permute-start = (bf16[1536,16]{0,1:T(8,128)(2,1)S(1)}, bf16[1536,16]{0,1:T(8,128)(2,1)S(1)}, u32[]{:S(2)}, u32[]{:S(2)}) collective-permute-start(bf16[1536,16]{0,1:T(8,128)(2,1)S(1)} %get-tuple-element.914), channel_id=1, source_target_pairs={{128,0},{256,128},{384,256},{129,1},{257,129},{385,257},{130,2},{2... | collective-permute-start | bytes 147464 | tf_op jit(solution)/shard_map/while/body/eval_jaxpr/ppermute | solution.py:14
  119.5 29.5 %copy-start.30 = (pred[256]{0:T(512)(128)(4,1)}, pred[256]{0:T(512)(128)(4,1)S(1)}, u32[]{:S(2)}) copy-start(pred[256]{0:T(512)(128)(4,1)S(1)} %compare_and_fusion.7) | copy-start | bytes 772 | tf_op jit(solution)/shard_map/while
  119.6 29.5 %copy-start.27 = (pred[256]{0:T(512)(128)(4,1)}, pred[256]{0:T(512)(128)(4,1)S(1)}, u32[]{:S(2)}) copy-start(pred[256]{0:T(512)(128)(4,1)S(1)} %compare_and_fusion.8) | copy-start | bytes 772 | tf_op jit(solution)/shard_map/while
  149.1 16.0 %copy-start.2 = (bf16[1,1,96,256]{3,2,1,0:T(8,128)(2,1)S(1)}, bf16[1,1,96,256]{3,2,1,0:T(8,128)(2,1)}, u32[]{:S(2)}) copy-start(bf16[1,1,96,256]{3,2,1,0:T(8,128)(2,1)} %get-tuple-element.978) | copy-start | bytes 147460 | tf_op jit(solution)/shard_map/while
  149.4 20.0 %copy-start.7 = (bf16[1,1,96,256]{3,2,1,0:T(8,128)(2,1)S(1)}, bf16[1,1,96,256]{3,2,1,0:T(8,128)(2,1)}, u32[]{:S(2)}) copy-start(bf16[1,1,96,256]{3,2,1,0:T(8,128)(2,1)} %get-tuple-element.981) | copy-start | bytes 147460 | tf_op jit(solution)/shard_map/while
  149.4 20.0 %copy-start.31 = (pred[256]{0:T(512)(128)(4,1)S(1)}, pred[256]{0:T(512)(128)(4,1)}, u32[]{:S(2)}) copy-start(pred[256]{0:T(512)(128)(4,1)} %copy-done.30) | copy-start | bytes 772 | tf_op jit(solution)/shard_map/while
  149.6 20.2 %copy-start.28 = (pred[256]{0:T(512)(128)(4,1)S(1)}, pred[256]{0:T(512)(128)(4,1)}, u32[]{:S(2)}) copy-start(pred[256]{0:T(512)(128)(4,1)} %copy-done.27) | copy-start | bytes 772 | tf_op jit(solution)/shard_map/while
  160.4 12.5 %all-to-all-start = ((bf16[16,96,16]{1,2,0:T(8,128)(2,1)}), bf16[16,96,16]{1,2,0:T(8,128)(2,1)S(1)}, u32[]{:S(2)}, u32[]{:S(2)}) async-start(bf16[16,96,16]{1,2,0:T(8,128)(2,1)} %constant_dynamic-update-slice_fusion.79), calls=%async_computation | async-start | bytes 131072 | tf_op jit(solution)/shard_map/while/body/eval_jaxpr/all_to_all | solution.py:88
  171.7 19.9 %copy-start.22 = (f32[96]{0:T(128)S(1)}, f32[96]{0:T(128)}, u32[]{:S(2)}) copy-start(f32[96]{0:T(128)} %mul.953) | copy-start | bytes 1156 | tf_op jit(solution)/shard_map/while
  195.7 15.9 %copy-start.6 = (bf16[1,1,96,256]{3,2,1,0:T(8,128)(2,1)S(1)}, bf16[1,1,96,256]{3,2,1,0:T(8,128)(2,1)}, u32[]{:S(2)}) copy-start(bf16[1,1,96,256]{3,2,1,0:T(8,128)(2,1)} %get-tuple-element.980) | copy-start | bytes 147460 | tf_op jit(solution)/shard_map/while
  207.0 14.7 %all-to-all-start.1 = ((bf16[16,96,16]{1,2,0:T(8,128)(2,1)}), bf16[16,96,16]{1,2,0:T(8,128)(2,1)S(1)}, u32[]{:S(2)}, u32[]{:S(2)}) async-start(bf16[16,96,16]{1,2,0:T(8,128)(2,1)} %constant_dynamic-update-slice_fusion.95), calls=%async_computation.1 | async-start | bytes 131072 | tf_op jit(solution)/shard_map/while/body/eval_jaxpr/all_to_all | solution.py:88
  221.0 6.3 %copy-start.10 = (f32[2,96]{1,0:T(2,128)S(1)}, f32[2,96]{1,0:T(2,128)}, u32[]{:S(2)}) copy-start(f32[2,96]{1,0:T(2,128)} %get-tuple-element.948) | copy-start | bytes 2308 | tf_op jit(solution)/shard_map/while
  221.0 6.3 %copy-start.13 = (f32[2,96]{1,0:T(2,128)S(1)}, f32[2,96]{1,0:T(2,128)}, u32[]{:S(2)}) copy-start(f32[2,96]{1,0:T(2,128)} %get-tuple-element.949) | copy-start | bytes 2308 | tf_op jit(solution)/shard_map/while
  221.0 6.3 %copy-start.23 = (f32[96]{0:T(128)S(1)}, f32[96]{0:T(128)}, u32[]{:S(2)}) copy-start(f32[96]{0:T(128)} %get-tuple-element.916) | copy-start | bytes 1156 | tf_op jit(solution)/shard_map/while
  221.0 6.3 %copy-start.24 = (f32[96]{0:T(128)S(1)}, f32[96]{0:T(128)}, u32[]{:S(2)}) copy-start(f32[96]{0:T(128)} %get-tuple-element.918) | copy-start | bytes 1156 | tf_op jit(solution)/shard_map/while
  221.0 6.3 %copy-start.25 = (f32[96]{0:T(128)S(1)}, f32[96]{0:T(128)}, u32[]{:S(2)}) copy-start(f32[96]{0:T(128)} %get-tuple-element.917) | copy-start | bytes 1156 | tf_op jit(solution)/shard_map/while
  221.7 7.6 %copy-start.4 = (f32[2,96,432]{1,2,0:T(8,128)}, f32[2,96,432]{1,2,0:T(8,128)S(1)}, u32[]{:S(2)}) copy-start(f32[2,96,432]{1,2,0:T(8,128)S(1)} %fusion.384) | copy-start | bytes 995332 | tf_op jit(solution)/shard_map/while
  223.3 6.0 %collective-permute-start = (bf16[1536,16]{0,1:T(8,128)(2,1)S(1)}, bf16[1536,16]{0,1:T(8,128)(2,1)S(1)}, u32[]{:S(2)}, u32[]{:S(2)}) collective-permute-start(bf16[1536,16]{0,1:T(8,128)(2,1)S(1)} %get-tuple-element.914), channel_id=1, source_target_pairs={{128,0},{256,128},{384,256},{129,1},{257,129},{385,257},{130,2},{2... | collective-permute-start | bytes 147464 | tf_op jit(solution)/shard_map/while/body/eval_jaxpr/ppermute | solution.py:14
  229.3 29.5 %copy-start.30 = (pred[256]{0:T(512)(128)(4,1)}, pred[256]{0:T(512)(128)(4,1)S(1)}, u32[]{:S(2)}) copy-start(pred[256]{0:T(512)(128)(4,1)S(1)} %compare_and_fusion.7) | copy-start | bytes 772 | tf_op jit(solution)/shard_map/while
  229.4 29.5 %copy-start.27 = (pred[256]{0:T(512)(128)(4,1)}, pred[256]{0:T(512)(128)(4,1)S(1)}, u32[]{:S(2)}) copy-start(pred[256]{0:T(512)(128)(4,1)S(1)} %compare_and_fusion.8) | copy-start | bytes 772 | tf_op jit(solution)/shard_map/while
  258.9 16.0 %copy-start.2 = (bf16[1,1,96,256]{3,2,1,0:T(8,128)(2,1)S(1)}, bf16[1,1,96,256]{3,2,1,0:T(8,128)(2,1)}, u32[]{:S(2)}) copy-start(bf16[1,1,96,256]{3,2,1,0:T(8,128)(2,1)} %get-tuple-element.978) | copy-start | bytes 147460 | tf_op jit(solution)/shard_map/while
  259.2 20.0 %copy-start.7 = (bf16[1,1,96,256]{3,2,1,0:T(8,128)(2,1)S(1)}, bf16[1,1,96,256]{3,2,1,0:T(8,128)(2,1)}, u32[]{:S(2)}) copy-start(bf16[1,1,96,256]{3,2,1,0:T(8,128)(2,1)} %get-tuple-element.981) | copy-start | bytes 147460 | tf_op jit(solution)/shard_map/while
  259.2 20.0 %copy-start.31 = (pred[256]{0:T(512)(128)(4,1)S(1)}, pred[256]{0:T(512)(128)(4,1)}, u32[]{:S(2)}) copy-start(pred[256]{0:T(512)(128)(4,1)} %copy-done.30) | copy-start | bytes 772 | tf_op jit(solution)/shard_map/while
  259.4 20.2 %copy-start.28 = (pred[256]{0:T(512)(128)(4,1)S(1)}, pred[256]{0:T(512)(128)(4,1)}, u32[]{:S(2)}) copy-start(pred[256]{0:T(512)(128)(4,1)} %copy-done.27) | copy-start | bytes 772 | tf_op jit(solution)/shard_map/while
  270.2 12.5 %all-to-all-start = ((bf16[16,96,16]{1,2,0:T(8,128)(2,1)}), bf16[16,96,16]{1,2,0:T(8,128)(2,1)S(1)}, u32[]{:S(2)}, u32[]{:S(2)}) async-start(bf16[16,96,16]{1,2,0:T(8,128)(2,1)} %constant_dynamic-update-slice_fusion.79), calls=%async_computation | async-start | bytes 131072 | tf_op jit(solution)/shard_map/while/body/eval_jaxpr/all_to_all | solution.py:88
  281.5 19.9 %copy-start.22 = (f32[96]{0:T(128)S(1)}, f32[96]{0:T(128)}, u32[]{:S(2)}) copy-start(f32[96]{0:T(128)} %mul.953) | copy-start | bytes 1156 | tf_op jit(solution)/shard_map/while
  305.5 15.9 %copy-start.6 = (bf16[1,1,96,256]{3,2,1,0:T(8,128)(2,1)S(1)}, bf16[1,1,96,256]{3,2,1,0:T(8,128)(2,1)}, u32[]{:S(2)}) copy-start(bf16[1,1,96,256]{3,2,1,0:T(8,128)(2,1)} %get-tuple-element.980) | copy-start | bytes 147460 | tf_op jit(solution)/shard_map/while
  316.8 14.7 %all-to-all-start.1 = ((bf16[16,96,16]{1,2,0:T(8,128)(2,1)}), bf16[16,96,16]{1,2,0:T(8,128)(2,1)S(1)}, u32[]{:S(2)}, u32[]{:S(2)}) async-start(bf16[16,96,16]{1,2,0:T(8,128)(2,1)} %constant_dynamic-update-slice_fusion.95), calls=%async_computation.1 | async-start | bytes 131072 | tf_op jit(solution)/shard_map/while/body/eval_jaxpr/all_to_all | solution.py:88
  330.8 6.3 %copy-start.10 = (f32[2,96]{1,0:T(2,128)S(1)}, f32[2,96]{1,0:T(2,128)}, u32[]{:S(2)}) copy-start(f32[2,96]{1,0:T(2,128)} %get-tuple-element.948) | copy-start | bytes 2308 | tf_op jit(solution)/shard_map/while
  330.8 6.3 %copy-start.13 = (f32[2,96]{1,0:T(2,128)S(1)}, f32[2,96]{1,0:T(2,128)}, u32[]{:S(2)}) copy-start(f32[2,96]{1,0:T(2,128)} %get-tuple-element.949) | copy-start | bytes 2308 | tf_op jit(solution)/shard_map/while
  331.5 7.6 %copy-start.4 = (f32[2,96,432]{1,2,0:T(8,128)}, f32[2,96,432]{1,2,0:T(8,128)S(1)}, u32[]{:S(2)}) copy-start(f32[2,96,432]{1,2,0:T(8,128)S(1)} %fusion.384) | copy-start | bytes 995332 | tf_op jit(solution)/shard_map/while
  333.1 6.0 %collective-permute-start = (bf16[1536,16]{0,1:T(8,128)(2,1)S(1)}, bf16[1536,16]{0,1:T(8,128)(2,1)S(1)}, u32[]{:S(2)}, u32[]{:S(2)}) collective-permute-start(bf16[1536,16]{0,1:T(8,128)(2,1)S(1)} %get-tuple-element.914), channel_id=1, source_target_pairs={{128,0},{256,128},{384,256},{129,1},{257,129},{385,257},{130,2},{2... | collective-permute-start | bytes 147464 | tf_op jit(solution)/shard_map/while/body/eval_jaxpr/ppermute | solution.py:14
  339.1 29.5 %copy-start.30 = (pred[256]{0:T(512)(128)(4,1)}, pred[256]{0:T(512)(128)(4,1)S(1)}, u32[]{:S(2)}) copy-start(pred[256]{0:T(512)(128)(4,1)S(1)} %compare_and_fusion.7) | copy-start | bytes 772 | tf_op jit(solution)/shard_map/while
  339.1 29.5 %copy-start.27 = (pred[256]{0:T(512)(128)(4,1)}, pred[256]{0:T(512)(128)(4,1)S(1)}, u32[]{:S(2)}) copy-start(pred[256]{0:T(512)(128)(4,1)S(1)} %compare_and_fusion.8) | copy-start | bytes 772 | tf_op jit(solution)/shard_map/while
  368.6 16.0 %copy-start.2 = (bf16[1,1,96,256]{3,2,1,0:T(8,128)(2,1)S(1)}, bf16[1,1,96,256]{3,2,1,0:T(8,128)(2,1)}, u32[]{:S(2)}) copy-start(bf16[1,1,96,256]{3,2,1,0:T(8,128)(2,1)} %get-tuple-element.978) | copy-start | bytes 147460 | tf_op jit(solution)/shard_map/while
  368.9 20.0 %copy-start.7 = (bf16[1,1,96,256]{3,2,1,0:T(8,128)(2,1)S(1)}, bf16[1,1,96,256]{3,2,1,0:T(8,128)(2,1)}, u32[]{:S(2)}) copy-start(bf16[1,1,96,256]{3,2,1,0:T(8,128)(2,1)} %get-tuple-element.981) | copy-start | bytes 147460 | tf_op jit(solution)/shard_map/while
  369.0 20.0 %copy-start.31 = (pred[256]{0:T(512)(128)(4,1)S(1)}, pred[256]{0:T(512)(128)(4,1)}, u32[]{:S(2)}) copy-start(pred[256]{0:T(512)(128)(4,1)} %copy-done.30) | copy-start | bytes 772 | tf_op jit(solution)/shard_map/while
  369.1 20.2 %copy-start.28 = (pred[256]{0:T(512)(128)(4,1)S(1)}, pred[256]{0:T(512)(128)(4,1)}, u32[]{:S(2)}) copy-start(pred[256]{0:T(512)(128)(4,1)} %copy-done.27) | copy-start | bytes 772 | tf_op jit(solution)/shard_map/while
  380.0 12.5 %all-to-all-start = ((bf16[16,96,16]{1,2,0:T(8,128)(2,1)}), bf16[16,96,16]{1,2,0:T(8,128)(2,1)S(1)}, u32[]{:S(2)}, u32[]{:S(2)}) async-start(bf16[16,96,16]{1,2,0:T(8,128)(2,1)} %constant_dynamic-update-slice_fusion.79), calls=%async_computation | async-start | bytes 131072 | tf_op jit(solution)/shard_map/while/body/eval_jaxpr/all_to_all | solution.py:88
  391.3 19.9 %copy-start.22 = (f32[96]{0:T(128)S(1)}, f32[96]{0:T(128)}, u32[]{:S(2)}) copy-start(f32[96]{0:T(128)} %mul.953) | copy-start | bytes 1156 | tf_op jit(solution)/shard_map/while
  415.3 15.9 %copy-start.6 = (bf16[1,1,96,256]{3,2,1,0:T(8,128)(2,1)S(1)}, bf16[1,1,96,256]{3,2,1,0:T(8,128)(2,1)}, u32[]{:S(2)}) copy-start(bf16[1,1,96,256]{3,2,1,0:T(8,128)(2,1)} %get-tuple-element.980) | copy-start | bytes 147460 | tf_op jit(solution)/shard_map/while
  426.6 14.7 %all-to-all-start.1 = ((bf16[16,96,16]{1,2,0:T(8,128)(2,1)}), bf16[16,96,16]{1,2,0:T(8,128)(2,1)S(1)}, u32[]{:S(2)}, u32[]{:S(2)}) async-start(bf16[16,96,16]{1,2,0:T(8,128)(2,1)} %constant_dynamic-update-slice_fusion.95), calls=%async_computation.1 | async-start | bytes 131072 | tf_op jit(solution)/shard_map/while/body/eval_jaxpr/all_to_all | solution.py:88
  440.5 6.3 %copy-start.10 = (f32[2,96]{1,0:T(2,128)S(1)}, f32[2,96]{1,0:T(2,128)}, u32[]{:S(2)}) copy-start(f32[2,96]{1,0:T(2,128)} %get-tuple-element.948) | copy-start | bytes 2308 | tf_op jit(solution)/shard_map/while
  440.6 6.3 %copy-start.13 = (f32[2,96]{1,0:T(2,128)S(1)}, f32[2,96]{1,0:T(2,128)}, u32[]{:S(2)}) copy-start(f32[2,96]{1,0:T(2,128)} %get-tuple-element.949) | copy-start | bytes 2308 | tf_op jit(solution)/shard_map/while
  441.3 7.6 %copy-start.4 = (f32[2,96,432]{1,2,0:T(8,128)}, f32[2,96,432]{1,2,0:T(8,128)S(1)}, u32[]{:S(2)}) copy-start(f32[2,96,432]{1,2,0:T(8,128)S(1)} %fusion.384) | copy-start | bytes 995332 | tf_op jit(solution)/shard_map/while
  442.9 6.0 %collective-permute-start = (bf16[1536,16]{0,1:T(8,128)(2,1)S(1)}, bf16[1536,16]{0,1:T(8,128)(2,1)S(1)}, u32[]{:S(2)}, u32[]{:S(2)}) collective-permute-start(bf16[1536,16]{0,1:T(8,128)(2,1)S(1)} %get-tuple-element.914), channel_id=1, source_target_pairs={{128,0},{256,128},{384,256},{129,1},{257,129},{385,257},{130,2},{2... | collective-permute-start | bytes 147464 | tf_op jit(solution)/shard_map/while/body/eval_jaxpr/ppermute | solution.py:14
  (69 other events, 164.5 us)
Sparse Core Ops, SparseCore 0:
  451.4 89.3 all-reduce.21
